TPU v7x, 32 devices: a whole 2x2x4 slice. The times are simulated.
32 devices in a mesh: row: 8 (over y, x, core), col: 4 (over z).
Axes of the slice: x: 2, y: 2, z: 4, core: 2. Of those that a mesh axis runs over, the one named last changes fastest.
Arguments:
- upper_blocks: bfloat16 [64, 8, 128, 128], P('row', None, 'col'), as said below
- block_cols: int32 [64, 8], replicated, may hold values from -1 to 63, as said below
- filter_cols: int32 [64, 8], replicated, may hold values from -1 to 63, as said below
Outputs:
- purified: float32 [64, 8, 128, 128], P('row', None, 'col')
Inputs may be any that keep to these rules, and one draw needn't show every extreme that they name: `block_cols`: slot 0 of row i holds i; every other slot holds -1 or a block column j with i < j < i + 8 and j < 64; the columns of a row are distinct; rows i <= 56 have no -1. `filter_cols`: slot 0 of row i holds i; every other slot holds -1 or a block column j with i < j < i + 8 and j < 64; the columns of a row are distinct; rows i <= 56 have no -1. Every diagonal block upper_blocks[i, 0] is symmetric.
All inputs are finite; a program needn't handle non-finite values.
Results may differ from a plain program's by a relative error of at most 0.002.
Values may be sent and summed in bfloat16 or wider, within the bound.
A program may use at most 128 MiB of HBM per device.

v0:
```python
import jax
import jax.numpy as jnp
from jax import lax
from jax.sharding import PartitionSpec as P

B = 128
W = 8


row_group = 4


def padded(value, sides, width):
    for axis, dim in sides:
        devices, length = (lax.axis_size(axis), value.shape[dim])
        up = [(i, (i + 1) % devices) for i in range(devices - 1)]
        down = [(j, i) for i, j in up]
        last = lax.slice_in_dim(value, length - width, length, axis=dim)
        leading = lax.slice_in_dim(value, 0, width, axis=dim)
        before = lax.ppermute(last, axis, up)
        after = lax.ppermute(leading, axis, down)
        value = jnp.concatenate([before, value, after], axis=dim)
    return value


def from_behind(value, axis, steps):
    count = lax.axis_size(axis)
    leading, last = (max(0, -steps), min(count, count - steps))
    return lax.ppermute(value, axis, [(source, source + steps) for source in range(leading, last)])


def band_right(blocks, columns, first_row):
    count_rows = blocks.shape[0]
    rim_rows = W - 1
    count_cols = count_rows - rim_rows
    first_col = first_row + rim_rows
    column_ids = first_col + jnp.arange(count_cols, dtype=jnp.int32)
    row_labels = first_row + jnp.arange(count_rows, dtype=jnp.int32)
    upper_hit = (columns[:, :, None] == column_ids[None, None, :]).astype(jnp.bfloat16)
    upper_part = jnp.einsum(
        "akxy,akb->axby", blocks, upper_hit, preferred_element_type=jnp.bfloat16
    )
    source = columns[rim_rows:]
    lower_hit = (source[:, :, None] == row_labels[None, None, :]) & (
        source[:, :, None] > column_ids[:, None, None]
    )
    lower_part = jnp.einsum(
        "bkxy,bka->aybx",
        blocks[rim_rows:],
        lower_hit.astype(jnp.bfloat16),
        preferred_element_type=jnp.bfloat16,
    )
    return upper_part + lower_part


def left_from_filter(own_slots, own_targets, mirror_slots, mirror_targets, first_row, row_count):
    rim_rows = W - 1
    count_cols = row_count + 2 * rim_rows
    band_ids = first_row + jnp.arange(count_cols, dtype=jnp.int32)
    own_ids = first_row + rim_rows + jnp.arange(row_count, dtype=jnp.int32)
    upper_hit = (own_targets[:, :, None] == band_ids[None, None, :]).astype(jnp.bfloat16)
    upper_part = jnp.einsum(
        "ifxy,ifa->ixay", own_slots, upper_hit, preferred_element_type=jnp.bfloat16
    )
    mirror_ids = first_row + jnp.arange(row_count + rim_rows, dtype=jnp.int32)
    lower_hit = (mirror_targets[:, :, None] == own_ids[None, None, :]) & (
        mirror_targets[:, :, None] > mirror_ids[:, None, None]
    )
    lower_part = jnp.einsum(
        "mfxy,mfi->ixmy",
        mirror_slots,
        lower_hit.astype(jnp.bfloat16),
        preferred_element_type=jnp.bfloat16,
    )
    lower_part = jnp.pad(lower_part, ((0, 0), (0, 0), (0, rim_rows), (0, 0)))
    return upper_part + lower_part


def pick_slots(product, targets, first_col):
    column_ids = first_col + jnp.arange(product.shape[2], dtype=jnp.int32)
    selector = (targets[:, :, None] == column_ids[None, None, :]).astype(jnp.float32)
    return jnp.einsum(
        "ixby,ifb->ifxy",
        product,
        selector,
        precision=lax.Precision.HIGHEST,
        preferred_element_type=jnp.float32,
    )


def group_products(left_rows, right_band, targets, first_col):
    outputs = []
    row_count = left_rows.shape[0]
    inner_rows = left_rows.shape[1]
    span_rows = row_group + 2 * (W - 1)
    width_cols = row_group + W - 1
    for group_index in range(row_count // row_group):
        row_start = group_index * row_group
        left_part = left_rows[
            row_start : row_start + row_group, :, row_start : row_start + span_rows, :
        ]
        left_part = left_part.reshape(row_group * inner_rows, span_rows * B)
        right_part = right_band[
            row_start : row_start + span_rows, :, row_start : row_start + width_cols, :
        ]
        right_part = right_part.reshape(span_rows * B, width_cols * B)
        product = jnp.dot(left_part, right_part, preferred_element_type=jnp.float32)
        product = product.reshape(row_group, inner_rows, width_cols, B)
        outputs.append(
            pick_slots(product, targets[row_start : row_start + row_group], first_col + row_start)
        )
    return jnp.concatenate(outputs, axis=0)


def per_device(upper_blocks, block_cols, filter_cols):
    rim_rows = W - 1
    row_count = upper_blocks.shape[0]
    quarter = upper_blocks.shape[2]
    row_first = lax.axis_index("row") * row_count
    col_first = lax.axis_index("col") * quarter
    padded_cols = jnp.pad(block_cols, ((rim_rows, rim_rows), (0, 0)), constant_values=-1)
    padded_filter = jnp.pad(filter_cols, ((rim_rows, 0), (0, 0)), constant_values=-1)
    window_cols = lax.dynamic_slice_in_dim(padded_cols, row_first, row_count + 2 * rim_rows, 0)
    window_filter = lax.dynamic_slice_in_dim(padded_filter, row_first, row_count + rim_rows, 0)
    own_filter = lax.dynamic_slice_in_dim(filter_cols, row_first, row_count, 0)
    whole_blocks = lax.all_gather(upper_blocks, "col", axis=2, tiled=True)
    window_blocks = padded(whole_blocks, (("row", 0),), rim_rows)
    band_first = row_first - rim_rows
    right_band = band_right(window_blocks, window_cols, band_first)
    own_band = lax.dynamic_slice_in_dim(right_band[:, :, :row_count, :], col_first, quarter, 3)
    left_rows = jnp.transpose(own_band, (2, 3, 0, 1))
    square = group_products(left_rows, right_band, own_filter, row_first)
    square_half = square.astype(jnp.bfloat16)
    whole_square = lax.all_gather(square_half, "col", axis=2, tiled=True)
    earlier = from_behind(whole_square[row_count - rim_rows :], "row", 1)
    joined = jnp.concatenate([earlier, whole_square], axis=0)
    mirror_cols = lax.dynamic_slice_in_dim(joined, col_first, quarter, 3)
    mirror_slots = jnp.swapaxes(mirror_cols, 2, 3)
    left_filter = left_from_filter(
        square_half, own_filter, mirror_slots, window_filter, band_first, row_count
    )
    cube_terms = group_products(left_filter, right_band, own_filter, row_first)
    return 3.0 * square - 2.0 * cube_terms


def solution(mesh):
    return jax.shard_map(
        per_device,
        mesh=mesh,
        in_specs=(P("row", None, "col", None), P(), P()),
        out_specs=P("row", None, "col", None),
        check_vma=False,
    )
```

profile of v0, /device:TPU:1, one launch (start us, length us, event | category | flops | bytes accessed | tf_op | source)
XLA Modules:
  0.0 326.4 jit_solution(9591159979319002050)
XLA Ops:
  8.7 48.3 %all-gather.3.cloned.1.call-done = bf16[8,8,128,128]{3,1,2,0:T(8,128)(2,1)} async-done(((bf16[8,8,32,128]{3,1,2,0:T(8,128)(2,1)}), bf16[8,8,128,128]{3,1,2,0:T(8,128)(2,1)}) %all-gather.3.cloned.1.call-update) | async-done | bytes 2097168 | tf_op jit(solution)/shard_map/all_gather | solution.py:126
  56.9 4.3 %fusion.70 = (bf16[7,8,128,128]{3,1,2,0:T(8,128)(2,1)}, bf16[7,8,128,128]{3,1,2,0:T(8,128)(2,1)}) fusion(bf16[8,8,128,128]{3,1,2,0:T(8,128)(2,1)} %all-gather.3.cloned.1.call-done), kind=kLoop, calls=%fused_computation.90 | loop fusion | bytes 7340032 | tf_op jit(solution)/shard_map/slice | solution.py:18
  67.7 34.4 %collective-permute-done.1 = bf16[7,8,128,128]{3,1,2,0:T(8,128)(2,1)} collective-permute-done((bf16[7,8,128,128]{3,1,2,0:T(8,128)(2,1)}, bf16[7,8,128,128]{3,1,2,0:T(8,128)(2,1)}, u32[]{:S(2)}, u32[]{:S(2)}) %collective-permute-start.1) | collective-permute-done | bytes 1835040 | tf_op jit(solution)/shard_map/ppermute | solution.py:21
  102.1 7.3 %fusion.7 = bf16[15,22,128,128]{3,1,2,0:T(8,128)(2,1)} fusion(bf16[7,8,128,128]{3,1,2,0:T(8,128)(2,1)} %collective-permute-done.1, bf16[8,8,128,128]{3,1,2,0:T(8,128)(2,1)S(1)} %copy-done, s32[22]{0:T(128)S(1)} %iota_add_fusion.3, s32[15,8]{1,0:T(8,128)S(1)} %copy.20, pred[15,8]{1,0:T(8,128)(4,1)S(1)} %copy.21), kind=kOutput, calls=%fused_computation.12 | convolution fusion | flops 94377120 | bytes 14746288 | tf_op jit(solution)/shard_map/bkxy,bka->aybx/dot_general | solution.py:47
  109.4 26.8 %copy.22 = bf16[15,22,128,128]{2,0,3,1:T(8,128)(2,1)} copy(bf16[15,22,128,128]{3,1,2,0:T(8,128)(2,1)} %fusion.7) | data formatting | bytes 21626880 | tf_op jit(solution)/shard_map/bkxy,bka->aybx/dot_general | solution.py:47
  136.3 8.0 %fusion = bf16[22,15,128,128]{3,1,2,0:T(8,128)(2,1)} fusion(bf16[7,8,128,128]{3,1,2,0:T(8,128)(2,1)} %collective-permute-done.1, bf16[8,8,128,128]{3,1,2,0:T(8,128)(2,1)S(1)} %copy-done, bf16[7,8,128,128]{3,1,2,0:T(8,128)(2,1)} %collective-permute-done, s32[15]{0:T(128)S(1)} %iota_add_fusion.4, s32[22,8]{1,0:T(8,128)S(1)} %copy.18), kind=kOutput, calls=%fused_computation.3 | convolution fusion | flops 103811664 | bytes 16581372 | tf_op jit(solution)/shard_map/akxy,akb->axby/dot_general | solution.py:40
  144.3 8.6 %bitcast_add_fusion = bf16[22,128,15,128]{3,2,1,0:T(8,128)(2,1)S(1)} fusion(bf16[15,22,128,128]{2,0,3,1:T(8,128)(2,1)} %copy.22, bf16[22,15,128,128]{3,1,2,0:T(8,128)(2,1)} %fusion), kind=kLoop, calls=%fused_computation | loop fusion | flops 5406720 | bytes 32440320 | tf_op jit(solution)/shard_map/add | solution.py:53
  152.9 3.6 %slice.60 = bf16[22,128,8,128]{3,2,1,0:T(8,128)(2,1)} slice(bf16[22,128,15,128]{3,2,1,0:T(8,128)(2,1)S(1)} %bitcast_add_fusion), slice={[0:22], [0:128], [0:8], [0:128]} | slice | bytes 11534336 | tf_op jit(solution)/shard_map/slice | solution.py:130
  156.5 6.9 %fusion.68 = (bf16[18,128,11,128]{3,2,1,0:T(8,128)(2,1)S(1)}, bf16[18,128,11,128]{3,2,1,0:T(8,128)(2,1)}) fusion(bf16[22,128,15,128]{3,2,1,0:T(8,128)(2,1)S(1)} %bitcast_add_fusion), kind=kLoop, calls=%fused_computation.88 | loop fusion | bytes 25952256 | tf_op jit(solution)/shard_map/slice | solution.py:103
  163.4 4.3 %dynamic-slice_bitcast_fusion = bf16[8,32,22,128]{1,0,3,2:T(8,128)(2,1)S(1)} fusion(bf16[22,128,8,128]{3,2,1,0:T(8,128)(2,1)} %slice.60, s32[]{:T(128)S(6)} %select_n.15), kind=kLoop, calls=%fused_computation.9 | loop fusion | bytes 2883588 | tf_op jit(solution)/shard_map/transpose | solution.py:131
  167.7 4.7 %fusion.69 = (bf16[4,32,18,128]{1,0,3,2:T(4,128)(2,1)}, bf16[4,32,18,128]{1,0,3,2:T(4,128)(2,1)}) fusion(bf16[8,32,22,128]{1,0,3,2:T(8,128)(2,1)S(1)} %dynamic-slice_bitcast_fusion), kind=kLoop, calls=%fused_computation.89 | loop fusion | bytes 2359296 | tf_op jit(solution)/shard_map/slice | solution.py:99
  172.4 6.0 %copy.66 = bf16[288,8,11,128]{3,1,2,0:T(8,128)(2,1)} copy(bf16[288,8,11,128]{3,2,1,0:T(8,128)(2,1)S(1)} %bitcast.86) | data formatting | bytes 12976128
  178.4 9.3 %copy.46 = bf16[2304,1408]{0,1:T(8,128)(2,1)} copy(bf16[2304,1408]{1,0:T(8,128)(2,1)} %bitcast.87) | data formatting | bytes 12976128 | tf_op jit(solution)/shard_map/reshape | solution.py:106
  187.7 9.7 %copy.65 = bf16[288,8,11,128]{3,1,2,0:T(8,128)(2,1)} copy(bf16[288,8,11,128]{3,2,1,0:T(8,128)(2,1)} %bitcast.85) | data formatting | bytes 12976128
  197.4 9.5 %copy.47 = bf16[2304,1408]{0,1:T(8,128)(2,1)} copy(bf16[2304,1408]{1,0:T(8,128)(2,1)} %bitcast.88) | data formatting | bytes 12976128 | tf_op jit(solution)/shard_map/reshape | solution.py:106
  206.9 6.5 %fusion.13 = f32[4,32,11,128]{3,1,2,0:T(8,128)S(1)} fusion(bf16[11,128,2304,1]{2,1,0,3:T(8,128)(2,1)} %bitcast.91, bf16[4,32,2304,1]{1,0,2,3:T(4,128)(2,1)S(1)} %bitcast.95), kind=kOutput, calls=%fused_computation.18 | convolution fusion | flops 830472192 | bytes 7798784 | tf_op jit(solution)/shard_map/dot_general | solution.py:107
  213.4 4.0 %fusion.11 = f32[4,32,11,128]{3,1,2,0:T(8,128)S(1)} fusion(bf16[11,128,2304,1]{2,1,0,3:T(8,128)(2,1)S(1)} %bitcast.90, bf16[4,32,2304,1]{1,0,2,3:T(4,128)(2,1)S(1)} %bitcast.94), kind=kOutput, calls=%fused_computation.16 | convolution fusion | flops 830472192 | bytes 7798784 | tf_op jit(solution)/shard_map/dot_general | solution.py:107
  220.0 46.2 %all-gather.5.cloned.1.call-done = bf16[8,8,128,128]{3,1,2,0:T(8,128)(2,1)} async-done(((bf16[8,8,32,128]{3,1,2,0:T(8,128)(2,1)}), bf16[8,8,128,128]{3,1,2,0:T(8,128)(2,1)}) %all-gather.5.cloned.1.call-update) | async-done | bytes 2097168 | tf_op jit(solution)/shard_map/all_gather | solution.py:134
  269.2 3.7 %collective-permute-start.2 = (bf16[7,8,128,128]{3,1,2,0:T(8,128)(2,1)}, bf16[7,8,128,128]{3,1,2,0:T(8,128)(2,1)}, u32[]{:S(2)}, u32[]{:S(2)}) collective-permute-start(bf16[7,8,128,128]{3,1,2,0:T(8,128)(2,1)} %slice.65), channel_id=1, source_target_pairs={{0,4},{4,8},{8,12},{12,16},{16,20},{20,24},{24,28},{1,5},{5,9},{9,... | collective-permute-start | bytes 5505032 | tf_op jit(solution)/shard_map/ppermute | solution.py:29
  273.2 20.1 %collective-permute-done.2 = bf16[7,8,128,128]{3,1,2,0:T(8,128)(2,1)} collective-permute-done((bf16[7,8,128,128]{3,1,2,0:T(8,128)(2,1)}, bf16[7,8,128,128]{3,1,2,0:T(8,128)(2,1)}, u32[]{:S(2)}, u32[]{:S(2)}) %collective-permute-start.2) | collective-permute-done | bytes 1835040 | tf_op jit(solution)/shard_map/ppermute | solution.py:29
  293.3 4.5 %fusion.6 = bf16[15,8,32,128]{2,1,3,0:T(8,128)(2,1)} fusion(s32[]{:T(128)S(6)} %select_n.15, bf16[8,8,128,128]{3,1,2,0:T(8,128)(2,1)S(1)} %copy-done.1, bf16[7,8,128,128]{3,1,2,0:T(8,128)(2,1)} %collective-permute-done.2), kind=kLoop, calls=%fused_computation.11 | loop fusion | flops 1966080 | bytes 4915204 | tf_op jit(solution)/shard_map/transpose | solution.py:138
  297.8 4.7 %copy.29 = bf16[15,8,32,128]{3,1,2,0:T(8,128)(2,1)S(1)} copy(bf16[15,8,32,128]{2,1,3,0:T(8,128)(2,1)} %fusion.6) | data formatting | bytes 1966080 | tf_op jit(solution)/shard_map/transpose | solution.py:138
  306.1 5.2 %fusion.27 = f32[4,32,11,128]{3,1,2,0:T(8,128)S(1)} fusion(bf16[11,128,2304,1]{2,1,0,3:T(8,128)(2,1)} %bitcast.92, bf16[4,32,2304,1]{2,1,0,3:T(8,128)(2,1)} %reshape.82), kind=kOutput, calls=%fused_computation.36 | convolution fusion | flops 830472192 | bytes 7798784 | tf_op jit(solution)/shard_map/dot_general | solution.py:107
  312.4 5.0 %fusion.25 = f32[4,32,11,128]{3,1,2,0:T(8,128)S(1)} fusion(bf16[11,128,2304,1]{2,1,0,3:T(8,128)(2,1)} %bitcast.89, bf16[4,32,2304,1]{2,1,0,3:T(8,128)(2,1)S(1)} %reshape.83), kind=kOutput, calls=%fused_computation.34 | convolution fusion | flops 830472192 | bytes 7798784 | tf_op jit(solution)/shard_map/dot_general | solution.py:107
  (58 shorter events, 21.2 us)
Async XLA Ops:
  6.5 50.4 %all-gather.3.cloned.1.call-start = ((), (), s32[]{:S(2)}) async-start(), calls=%async_computation | async-start | bytes 2621440 | tf_op jit(solution)/shard_map/all_gather | solution.py:126
  8.6 58.3 %copy-start.7 = (s32[64,8]{0,1:T(8,128)S(1)}, s32[64,8]{0,1:T(8,128)}, u32[]{:S(2)}) copy-start(s32[64,8]{0,1:T(8,128)} %param.4) | copy-start | bytes 6148
  8.6 58.8 %copy-start.6 = (s32[64,8]{0,1:T(8,128)S(1)}, s32[64,8]{0,1:T(8,128)}, u32[]{:S(2)}) copy-start(s32[64,8]{0,1:T(8,128)} %param.5) | copy-start | bytes 6148
  8.6 257.6 %all-gather.5.cloned.1.call-start = ((), (), s32[]{:S(2)}) async-start(), calls=%async_computation.1 | async-start | bytes 2621440 | tf_op jit(solution)/shard_map/all_gather | solution.py:134
  56.9 45.2 %copy-start = (bf16[8,8,128,128]{3,1,2,0:T(8,128)(2,1)S(1)}, bf16[8,8,128,128]{3,1,2,0:T(8,128)(2,1)}, u32[]{:S(2)}) copy-start(bf16[8,8,128,128]{3,1,2,0:T(8,128)(2,1)} %all-gather.3.cloned.1.call-done) | copy-start | bytes 6291460
  61.3 40.8 %collective-permute-start.1 = (bf16[7,8,128,128]{3,1,2,0:T(8,128)(2,1)}, bf16[7,8,128,128]{3,1,2,0:T(8,128)(2,1)}, u32[]{:S(2)}, u32[]{:S(2)}) collective-permute-start(bf16[7,8,128,128]{3,1,2,0:T(8,128)(2,1)} %get-tuple-element.12), channel_id=1, source_target_pairs={{4,0},{8,4},{12,8},{16,12},{20,16},{24,20},{28,24},{5,1},{9,5},{13... | collective-permute-start | bytes 5505032 | tf_op jit(solution)/shard_map/ppermute | solution.py:21
  63.9 72.4 %collective-permute-start = (bf16[7,8,128,128]{3,1,2,0:T(8,128)(2,1)}, bf16[7,8,128,128]{3,1,2,0:T(8,128)(2,1)}, u32[]{:S(2)}, u32[]{:S(2)}) collective-permute-start(bf16[7,8,128,128]{3,1,2,0:T(8,128)(2,1)} %get-tuple-element.11), channel_id=1, source_target_pairs={{0,4},{4,8},{8,12},{12,16},{16,20},{20,24},{24,28},{1,5},{5,9},{9,... | collective-permute-start | bytes 5505032 | tf_op jit(solution)/shard_map/ppermute | solution.py:20
  197.4 9.5 %copy-start.5 = (bf16[4,32,18,128]{1,0,3,2:T(4,128)(2,1)S(1)}, bf16[4,32,18,128]{1,0,3,2:T(4,128)(2,1)}, u32[]{:S(2)}) copy-start(bf16[4,32,18,128]{1,0,3,2:T(4,128)(2,1)} %get-tuple-element.9) | copy-start | bytes 1769476
  206.9 6.5 %copy-start.2 = (bf16[2304,1408]{0,1:T(8,128)(2,1)S(1)}, bf16[2304,1408]{0,1:T(8,128)(2,1)}, u32[]{:S(2)}) copy-start(bf16[2304,1408]{0,1:T(8,128)(2,1)} %copy.47) | copy-start | bytes 19464196
  206.9 6.5 %copy-start.4 = (bf16[4,32,18,128]{1,0,3,2:T(4,128)(2,1)S(1)}, bf16[4,32,18,128]{1,0,3,2:T(4,128)(2,1)}, u32[]{:S(2)}) copy-start(bf16[4,32,18,128]{1,0,3,2:T(4,128)(2,1)} %get-tuple-element.10) | copy-start | bytes 1769476
  266.2 27.2 %copy-start.1 = (bf16[8,8,128,128]{3,1,2,0:T(8,128)(2,1)S(1)}, bf16[8,8,128,128]{3,1,2,0:T(8,128)(2,1)}, u32[]{:S(2)}) copy-start(bf16[8,8,128,128]{3,1,2,0:T(8,128)(2,1)} %all-gather.5.cloned.1.call-done) | copy-start | bytes 6291460
  269.2 24.2 %collective-permute-start.2 = (bf16[7,8,128,128]{3,1,2,0:T(8,128)(2,1)}, bf16[7,8,128,128]{3,1,2,0:T(8,128)(2,1)}, u32[]{:S(2)}, u32[]{:S(2)}) collective-permute-start(bf16[7,8,128,128]{3,1,2,0:T(8,128)(2,1)} %slice.65), channel_id=1, source_target_pairs={{0,4},{4,8},{8,12},{12,16},{16,20},{20,24},{24,28},{1,5},{5,9},{9,... | collective-permute-start | bytes 5505032 | tf_op jit(solution)/shard_map/ppermute | solution.py:29
  297.8 5.9 %copy-start.3 = (bf16[8,8,32,128]{3,1,2,0:T(8,128)(2,1)S(1)}, bf16[8,8,32,128]{3,1,2,0:T(8,128)(2,1)}, u32[]{:S(2)}) copy-start(bf16[8,8,32,128]{3,1,2,0:T(8,128)(2,1)} %fusion.24) | copy-start | bytes 1572868
Sparse Core Ops, SparseCore 0:
  8.9 47.9 all-gather.2
  220.1 46.0 all-gather.4
where the time goes:
time: 328 us; the launch traced here: 326 us
  waiting for transfers between devices  149 us (45%)
  local copies, waits for them, and re-layouts  99.6 us (30%)
  matrix products  40.7 us (12%)
  other arithmetic  14.2 us (4%)
  between operations  13.6 us (4%)
  starting transfers between devices  9.34 us (3%)
    all_gather x1, waiting for transfers between devices, per_device(): whole_blocks = lax.all_gather(upper_blocks, 'col', axis=2, tiled=True)  48.3 us
    all_gather x1, waiting for transfers between devices, per_device(): whole_square = lax.all_gather(square_half, 'col', axis=2, tiled=True)  46.2 us
    ppermute x1, waiting for transfers between devices, padded(): after = lax.ppermute(leading, axis, down)  34.4 us
    dot_general x1, local copies, waits for them, and re-layouts, band_right(): jnp.einsum('bkxy,bka->aybx', blocks[rim_rows:], lower_hit.astype(jnp.bflo...  26.8 us
    dot_general x4, matrix products, group_products(): product = jnp.dot(left_part, right_part, preferred_element_type=jnp.float32)  20.7 us
    ppermute x1, waiting for transfers between devices, from_behind(): lax.ppermute(value, axis, [(source, source + steps) for source in range(l...  20.1 us
    reshape x2, local copies, waits for them, and re-layouts, group_products(): right_part = right_part.reshape(span_rows * B, width_cols * B)  18.8 us
    unnamed x19, local copies, waits for them, and re-layouts  17.8 us
  transfers between devices with their start and end apart: 5, of which 4 were waited for; matrix products, arithmetic and copies ran while one was open for 11% of the time, Pallas kernels for 0%

commit v1 on v0

v1 whole, which is shorter than its diff:
```python
import functools

import jax
import jax.numpy as jnp
from jax import lax
from jax.experimental import pallas as pl
from jax.experimental.pallas import tpu as pltpu
from jax.sharding import PartitionSpec as P

B = 128
W = 8
RIM = W - 1
MESH = pl.DeviceIdType.MESH
NT = (((1,), (1,)), ((), ()))


def band_kernel(cols, slots, out):
    rows, kinds = slots.shape[0], slots.shape[1]
    first = lax.axis_index("row") * rows
    out[...] = jnp.zeros_like(out)
    for i in range(rows):
        for k in range(kinds):
            column = cols[first + i, k]

            @pl.when(column >= 0)
            def _(i=i, k=k, column=column):
                out[i, column - first - i] = slots[i, k]


def gather_kernel(
    row_devices, col_devices, own, window, local_sem, col_send, col_recv, row_send, row_recv
):
    rows = own.shape[0]
    r, q = lax.axis_index("row"), lax.axis_index("col")
    has_next, has_before = r < row_devices - 1, r > 0
    has_up, has_down = q < col_devices - 1, q > 0
    next_row, before_row = {"row": r + 1}, {"row": r - 1}
    up_col, down_col = {"col": q + 1}, {"col": q - 1}
    neighbours = (
        (has_next, next_row), (has_before, before_row), (has_up, up_col), (has_down, down_col)
    )

    barrier = pltpu.get_barrier_semaphore()
    count = jnp.int32(0)
    for present, device in neighbours:

        @pl.when(present)
        def _(device=device):
            pl.semaphore_signal(barrier, inc=1, device_id=device, device_id_type=MESH)

        count = count + present.astype(jnp.int32)
    pl.semaphore_wait(barrier, count)

    local = pltpu.make_async_copy(own, window.at[q, RIM : RIM + rows], local_sem)
    local.start()

    def source(shard, is_own):
        return own if is_own else window.at[shard, RIM : RIM + rows]

    def col_copy(shard, is_own, up, step):
        return pltpu.make_async_remote_copy(
            src_ref=source(shard, is_own),
            dst_ref=window.at[shard, RIM : RIM + rows],
            send_sem=col_send.at[0 if up else 1, step],
            recv_sem=col_recv.at[shard],
            device_id=up_col if up else down_col,
            device_id_type=MESH,
        )

    def halo_copies(shard, is_own, onward):
        src = source(shard, is_own)
        if onward:
            parts = (((rows - RIM, rows), (0, W), 0, 0),)
            device = next_row
        else:
            parts = (
                ((0, 4), (0, RIM), RIM + rows, 1),
                ((4, RIM), (0, 3), RIM + rows + 4, 2),
            )
            device = before_row
        return [
            pltpu.make_async_remote_copy(
                src_ref=src.at[lo:hi, kinds[0] : kinds[1]],
                dst_ref=window.at[shard, place : place + hi - lo, kinds[0] : kinds[1]],
                send_sem=row_send.at[part, shard],
                recv_sem=row_recv.at[part, shard],
                device_id=device,
                device_id_type=MESH,
            )
            for (lo, hi), kinds, place, part in parts
        ]

    def spread(shard, is_own):
        for present, onward in ((has_next, True), (has_before, False)):

            @pl.when(present)
            def _(onward=onward):
                for copy in halo_copies(shard, is_own, onward):
                    copy.start()

    @pl.when(has_up)
    def _():
        col_copy(q, True, True, 0).start()

    @pl.when(has_down)
    def _():
        col_copy(q, True, False, 0).start()

    spread(q, True)

    for step in range(1, col_devices):
        for up in (True, False):
            shard = q - step if up else q + step
            arrives = shard >= 0 if up else shard < col_devices
            onward = has_up if up else has_down

            @pl.when(arrives)
            def _(shard=shard, up=up, onward=onward, step=step):
                col_copy(shard, False, up, step).wait_recv()

                @pl.when(onward)
                def _():
                    col_copy(shard, False, up, step).start()

                spread(shard, False)

    local.wait()
    for step in range(col_devices):
        for up in (True, False):
            shard = q - step if up else q + step
            arrives = shard >= 0 if up else shard < col_devices
            onward = has_up if up else has_down

            @pl.when(arrives & onward)
            def _(shard=shard, up=up, step=step):
                col_copy(shard, step == 0, up, step).wait_send()

    for shard in range(col_devices):

        @pl.when(has_next)
        def _(shard=shard):
            for copy in halo_copies(shard, False, True):
                copy.wait_send()
            for copy in halo_copies(shard, False, False):
                copy.wait_recv()

        @pl.when(has_before)
        def _(shard=shard):
            for copy in halo_copies(shard, False, False):
                copy.wait_send()
            for copy in halo_copies(shard, False, True):
                copy.wait_recv()


def product_kernel(
    row_devices, rows, quarter, targets, keep, window, out, blocks, left, filtered, held, sem
):
    span = rows + 2 * RIM
    devices = B // quarter
    r, q = lax.axis_index("row"), lax.axis_index("col")
    base = RIM

    def fetch(start):
        def go(lo, hi, kinds, part):
            for shard in range(devices):
                copy = pltpu.make_async_copy(
                    window.at[shard, lo:hi, 0:kinds],
                    blocks.at[base + lo : base + hi, 0:kinds, shard * quarter : (shard + 1) * quarter],
                    sem.at[part, shard],
                )
                copy.start() if start else copy.wait()

        go(RIM, RIM + rows, W, 0)

        @pl.when(r > 0)
        def _():
            go(0, RIM, W, 1)

        @pl.when(r < row_devices - 1)
        def _():
            go(RIM + rows, RIM + rows + 4, RIM, 2)
            go(RIM + rows + 4, span, 3, 3)

    blocks[0:RIM] = jnp.zeros((RIM,) + blocks.shape[1:], blocks.dtype)
    after = base + RIM + rows
    blocks[after : after + 4, RIM:W] = jnp.zeros((4, 1, B, B), blocks.dtype)
    blocks[after + 4 : after + RIM, 3:W] = jnp.zeros((3, W - 3, B, B), blocks.dtype)

    @pl.when(r == 0)
    def _():
        blocks[RIM : 2 * RIM] = jnp.zeros((RIM,) + blocks.shape[1:], blocks.dtype)

    @pl.when(r == row_devices - 1)
    def _():
        blocks[after : after + 4, 0:RIM] = jnp.zeros((4, RIM, B, B), blocks.dtype)
        blocks[after + 4 : after + RIM, 0:3] = jnp.zeros((3, 3, B, B), blocks.dtype)

    fetch(True)
    left[...] = jnp.zeros_like(left)
    filtered[...] = jnp.zeros_like(filtered)
    fetch(False)

    places = lax.broadcasted_iota(jnp.int32, (quarter, B), 0) + q * quarter
    select = (places == lax.broadcasted_iota(jnp.int32, (quarter, B), 1)).astype(jnp.bfloat16)
    own = pl.ds(pl.multiple_of(q * quarter, quarter), quarter)

    @pl.loop(0, rows)
    def _(i):
        strip = pl.ds(pl.multiple_of(i * quarter, quarter), quarter)
        at = base + RIM + i
        for d in range(W):
            left[at + d, strip, :] = blocks[at, d, own, :]
        for d in range(1, W):
            left[at - d, strip, :] = lax.dot_general(
                select, blocks[at - d, d], NT, preferred_element_type=jnp.float32
            ).astype(jnp.bfloat16)

    def column(lhs, c):
        at = base + c
        low_l = jnp.concatenate([lhs[at - d] for d in range(1, W)], axis=1)
        low_r = jnp.concatenate([blocks[at - d, d] for d in range(1, W)], axis=0)
        high_l = jnp.concatenate([lhs[at + d] for d in range(W)], axis=1)
        high_r = jnp.concatenate([blocks[at, d] for d in range(W)], axis=1)
        total = jnp.dot(low_l, low_r, preferred_element_type=jnp.float32)
        return total + lax.dot_general(
            high_l, high_r, NT, preferred_element_type=jnp.float32
        )

    @pl.loop(0, span)
    def _(c):
        square = column(left, c)
        for i in range(rows):
            piece = square[i * quarter : (i + 1) * quarter]
            kept = keep[i, c] != 0
            filtered[base + c, i * quarter : (i + 1) * quarter, :] = jnp.where(
                kept, piece, 0.0
            ).astype(jnp.bfloat16)
            offset = c - RIM - i

            @pl.when((offset >= 0) & (offset < W))
            def _(i=i, piece=piece, offset=offset):
                held[i, offset] = 3.0 * piece

    @pl.loop(RIM, span)
    def _(c):
        cube = column(filtered, c)
        for i in range(rows):
            piece = cube[i * quarter : (i + 1) * quarter]
            offset = c - RIM - i

            @pl.when((offset >= 0) & (offset < W))
            def _(i=i, piece=piece, offset=offset):
                held[i, offset] = held[i, offset] - 2.0 * piece

    first = r * rows
    for i in range(rows):
        for f in range(out.shape[1]):
            target = targets[first + i, f]
            there = target >= 0
            offset = jnp.where(there, target - first - i, 0)
            out[i, f] = jnp.where(there, held[i, offset], 0.0)


def per_device(row_devices, col_devices, upper_blocks, block_cols, filter_cols):
    rows, kinds, quarter, _ = upper_blocks.shape
    span = rows + 2 * RIM
    row_first = lax.axis_index("row") * rows

    own_ids = row_first + jnp.arange(rows, dtype=jnp.int32)
    span_ids = row_first - RIM + jnp.arange(span, dtype=jnp.int32)
    own_filter = lax.dynamic_slice_in_dim(filter_cols, row_first, rows, 0)
    padded_filter = jnp.pad(filter_cols, ((RIM, RIM), (0, 0)), constant_values=-1)
    span_filter = lax.dynamic_slice_in_dim(padded_filter, row_first, span, 0)
    upper = jnp.any(own_filter[:, None, :] == span_ids[None, :, None], axis=2)
    upper = upper & (span_ids >= 0)[None, :]
    lower = jnp.any(span_filter[None, :, :] == own_ids[:, None, None], axis=2)
    keep = (upper | lower).astype(jnp.int32)

    vmem = pl.BlockSpec(memory_space=pltpu.VMEM)
    smem = pl.BlockSpec(memory_space=pltpu.SMEM)
    anywhere = pl.BlockSpec(memory_space=pl.ANY)
    band = pl.pallas_call(
        band_kernel,
        out_shape=jax.ShapeDtypeStruct((rows, W, quarter, B), jnp.bfloat16),
        in_specs=[smem, vmem],
        out_specs=vmem,
        name="band_order",
    )(block_cols, upper_blocks)
    window = pl.pallas_call(
        functools.partial(gather_kernel, row_devices, col_devices),
        out_shape=jax.ShapeDtypeStruct((col_devices, span, W, quarter, B), jnp.bfloat16),
        in_specs=[anywhere],
        out_specs=anywhere,
        scratch_shapes=[
            pltpu.SemaphoreType.DMA,
            pltpu.SemaphoreType.DMA((2, col_devices)),
            pltpu.SemaphoreType.DMA((col_devices,)),
            pltpu.SemaphoreType.DMA((3, col_devices)),
            pltpu.SemaphoreType.DMA((3, col_devices)),
        ],
        compiler_params=pltpu.CompilerParams(collective_id=0, has_side_effects=True),
        name="gather_window",
    )(band)
    return pl.pallas_call(
        functools.partial(product_kernel, row_devices, rows, quarter),
        out_shape=jax.ShapeDtypeStruct((rows, filter_cols.shape[1], quarter, B), jnp.float32),
        in_specs=[smem, smem, anywhere],
        out_specs=vmem,
        scratch_shapes=[
            pltpu.VMEM((span + RIM, W, B, B), jnp.bfloat16),
            pltpu.VMEM((span + 2 * RIM, rows * quarter, B), jnp.bfloat16),
            pltpu.VMEM((span + 2 * RIM, rows * quarter, B), jnp.bfloat16),
            pltpu.VMEM((rows, W, quarter, B), jnp.float32),
            pltpu.SemaphoreType.DMA((4, col_devices)),
        ],
        compiler_params=pltpu.CompilerParams(vmem_limit_bytes=40 << 20),
        name="products",
    )(filter_cols, keep, window)


def solution(mesh):
    return jax.shard_map(
        functools.partial(per_device, mesh.shape["row"], mesh.shape["col"]),
        mesh=mesh,
        in_specs=(P("row", None, "col", None), P(), P()),
        out_specs=P("row", None, "col", None),
        check_vma=False,
    )
```

time: 328 us -> 86.8 us (0.26)
  waiting for transfers between devices: 149 us -> 0 us
  local copies, waits for them, and re-layouts: 99.6 us -> 6.37 us
  Pallas kernels: 0 us -> 79.9 us
  matrix products: 40.7 us -> 0 us
  other arithmetic: 14.2 us -> 0.12 us
  between operations: 13.6 us -> 0.04 us
  starting transfers between devices: 9.34 us -> 0 us
    all_gather x2 -> x0, waiting for transfers between devices: 94.5 us -> none  [the longest x1 48.3 us: per_device(): whole_blocks = lax.all_gather(upper_blocks, 'col', axis=2, tiled=True)]
    pallas_call x0 -> x3, Pallas kernels: none -> 79.9 us  [the longest x1 53.7 us: per_device(): pl.pallas_call(functools.partial(gather_kernel, row_devices, col_devices)...]
    ppermute x3 -> x0, waiting for transfers between devices: 54.5 us -> none  [the longest x1 34.4 us: padded(): after = lax.ppermute(leading, axis, down)]
    dot_general x12 -> x0, matrix products: 40.7 us -> none  [the longest x4 20.7 us: group_products(): product = jnp.dot(left_part, right_part, preferred_element_type=jnp.float32)]
    dot_general x4 -> x0, local copies, waits for them, and re-layouts: 28.9 us -> none  [the longest x1 26.8 us: band_right(): jnp.einsum('bkxy,bka->aybx', blocks[rim_rows:], lower_hit.astype(jnp.bflo...]
    slice x11 -> x0, local copies, waits for them, and re-layouts: 23.4 us -> none  [the longest x1 6.92 us: group_products(): right_band[row_start:row_start + span_rows, :, row_start:row_start + widt...]
    reshape x2 -> x0, local copies, waits for them, and re-layouts: 18.8 us -> none  [group_products(): right_part = right_part.reshape(span_rows * B, width_cols * B)]
    unnamed x19 -> x4, local copies, waits for them, and re-layouts: 17.8 us -> 4.77 us
  transfers between devices with their start and end apart: 5 -> 0, of which waited for: 4 -> 0; matrix products, arithmetic and copies ran while one was open for 11% -> 0% of each run, Pallas kernels for 0% -> 0%
where the time goes in v1:
time: 86.8 us; the launch traced here: 86.5 us
  Pallas kernels  79.9 us (92%)
  local copies, waits for them, and re-layouts  6.37 us (7%)
    pallas_call x1, Pallas kernels, per_device(): pl.pallas_call(functools.partial(gather_kernel, row_devices, col_devices)...  53.7 us
    pallas_call x1, Pallas kernels, per_device(): pl.pallas_call(functools.partial(product_kernel, row_devices, rows, quart...  23.7 us
    unnamed x4, local copies, waits for them, and re-layouts  4.77 us
    pallas_call x1, Pallas kernels, per_device(): pl.pallas_call(band_kernel, out_shape=jax.ShapeDtypeStruct((rows, W, quar...  2.55 us

profile of v1, /device:TPU:1, one launch (start us, length us, event | category | flops | bytes accessed | tf_op | source)
XLA Modules:
  0.0 86.5 jit_solution(5641106807531015886)
XLA Ops:
  0.0 0.8 constant_dynamic-slice_fusion
  0.8 0.1 copy.8
  0.9 0.8 pad_dynamic-slice_fusion
  1.6 0.1 compare_reduce_fusion
  1.7 1.4 %copy.9.cols = s32[64,8]{1,0:T(8,128)} copy(s32[64,8]{0,1:T(8,128)} %param.4) | data formatting | bytes 4096 | tf_op args[1]
  3.1 0.8 copy.10.targets
  3.9 2.6 %band_order.1.own = bf16[8,8,32,128]{3,2,1,0:T(8,128)(2,1)} custom-call(s32[64,8]{1,0:T(8,128)} %copy.9.cols, bf16[8,8,32,128]{3,2,1,0:T(8,128)(2,1)} %slots.1), custom_call_target="tpu_custom_call" | custom-call | tf_op jit(solution)/shard_map/band_order/pallas_call | solution.py:282
  6.4 53.7 %gather_window.1.window = bf16[4,22,8,32,128]{4,3,2,1,0:T(8,128)(2,1)} custom-call(bf16[8,8,32,128]{3,2,1,0:T(8,128)(2,1)} %band_order.1.own), custom_call_target="tpu_custom_call" | custom-call | tf_op jit(solution)/shard_map/gather_window/pallas_call | solution.py:289
  60.1 0.0 copy-start
  60.1 2.6 %copy-done = bf16[4,22,8,32,128]{4,3,2,1,0:T(8,128)(2,1)S(1)} copy-done((bf16[4,22,8,32,128]{4,3,2,1,0:T(8,128)(2,1)S(1)}, bf16[4,22,8,32,128]{4,3,2,1,0:T(8,128)(2,1)}, u32[]{:S(2)}) %copy-start) | copy-done | bytes 5767192
  62.7 23.7 %products.1 = f32[8,8,32,128]{3,2,1,0:T(8,128)} custom-call(s32[64,8]{1,0:T(8,128)S(1)} %copy.10.targets, s32[8,22]{1,0:T(8,128)S(1)} %or_convert_fusion.keep, bf16[4,22,8,32,128]{4,3,2,1,0:T(8,128)(2,1)S(1)} %copy-done), custom_call_target="tpu_custom_call" | custom-call | tf_op jit(solution)/shard_map/products/pallas_call | solution.py:304
  (4 shorter events, 0.0 us)
Async XLA Ops:
  60.1 2.6 %copy-start = (bf16[4,22,8,32,128]{4,3,2,1,0:T(8,128)(2,1)S(1)}, bf16[4,22,8,32,128]{4,3,2,1,0:T(8,128)(2,1)}, u32[]{:S(2)}) copy-start(bf16[4,22,8,32,128]{4,3,2,1,0:T(8,128)(2,1)} %gather_window.1.window) | copy-start | bytes 17301508

commit v2 on v1

v2 whole, which is shorter than its diff:
```python
import functools

import jax
import jax.numpy as jnp
from jax import lax
from jax.experimental import pallas as pl
from jax.experimental.pallas import tpu as pltpu
from jax.sharding import PartitionSpec as P

B = 128
W = 8
RIM = W - 1
MESH = pl.DeviceIdType.MESH
NT = (((1,), (1,)), ((), ()))


def row_chunks(rows):
    return [(lo, lo + 2) for lo in reversed(range(0, rows, 2))]


def band_kernel(cols, slots, out):
    rows, kinds = slots.shape[0], slots.shape[1]
    first = lax.axis_index("row") * rows
    out[...] = jnp.zeros_like(out)
    for i in range(rows):
        for k in range(kinds):
            column = cols[first + i, k]

            @pl.when(column >= 0)
            def _(i=i, k=k, column=column):
                out[i, column - first - i] = slots[i, k]


def gather_kernel(
    row_devices, col_devices, own, window, local_sem, col_send, col_recv, row_send, row_recv
):
    rows = own.shape[0]
    r, q = lax.axis_index("row"), lax.axis_index("col")
    has_next, has_before = r < row_devices - 1, r > 0
    has_up, has_down = q < col_devices - 1, q > 0
    next_row, before_row = {"row": r + 1}, {"row": r - 1}
    up_col, down_col = {"col": q + 1}, {"col": q - 1}
    neighbours = (
        (has_next, next_row), (has_before, before_row), (has_up, up_col), (has_down, down_col)
    )

    barrier = pltpu.get_barrier_semaphore()
    count = jnp.int32(0)
    for present, device in neighbours:

        @pl.when(present)
        def _(device=device):
            pl.semaphore_signal(barrier, inc=1, device_id=device, device_id_type=MESH)

        count = count + present.astype(jnp.int32)
    pl.semaphore_wait(barrier, count)

    local = pltpu.make_async_copy(own, window.at[q, RIM : RIM + rows], local_sem)
    local.start()
    chunks = row_chunks(rows)

    def source(shard, is_own, lo, hi):
        return own.at[lo:hi] if is_own else window.at[shard, RIM + lo : RIM + hi]

    def col_copy(shard, is_own, up, step, n):
        lo, hi = chunks[n]
        return pltpu.make_async_remote_copy(
            src_ref=source(shard, is_own, lo, hi),
            dst_ref=window.at[shard, RIM + lo : RIM + hi],
            send_sem=col_send.at[0 if up else 1, step, n],
            recv_sem=col_recv.at[shard, n],
            device_id=up_col if up else down_col,
            device_id_type=MESH,
        )

    def halo_copy(shard, is_own, onward, n):
        lo, hi = chunks[n]
        if onward:
            lo, kinds = max(lo, rows - RIM), W
            place, device = lo - (rows - RIM), next_row
        else:
            hi, kinds = min(hi, RIM), RIM - lo
            place, device = RIM + rows + lo, before_row
        return pltpu.make_async_remote_copy(
            src_ref=source(shard, is_own, lo, hi).at[:, 0:kinds],
            dst_ref=window.at[shard, place : place + hi - lo, 0:kinds],
            send_sem=row_send.at[0 if onward else 1, shard, n],
            recv_sem=row_recv.at[0 if onward else 1, shard, n],
            device_id=device,
            device_id_type=MESH,
        )

    def spread(shard, is_own, n):
        @pl.when(has_next)
        def _():
            halo_copy(shard, is_own, True, n).start()

        @pl.when(has_before)
        def _():
            halo_copy(shard, is_own, False, n).start()

    for n in range(len(chunks)):

        @pl.when(has_up)
        def _(n=n):
            col_copy(q, True, True, 0, n).start()

        @pl.when(has_down)
        def _(n=n):
            col_copy(q, True, False, 0, n).start()

        spread(q, True, n)

    for step in range(1, col_devices):
        for n in range(len(chunks)):
            for up in (True, False):
                shard = q - step if up else q + step
                arrives = shard >= 0 if up else shard < col_devices
                onward = has_up if up else has_down

                @pl.when(arrives)
                def _(shard=shard, up=up, onward=onward, step=step, n=n):
                    col_copy(shard, False, up, step, n).wait_recv()

                    @pl.when(onward)
                    def _():
                        col_copy(shard, False, up, step, n).start()

                    spread(shard, False, n)

    local.wait()
    for step in range(col_devices):
        for up in (True, False):
            shard = q - step if up else q + step
            arrives = shard >= 0 if up else shard < col_devices
            onward = has_up if up else has_down

            @pl.when(arrives & onward)
            def _(shard=shard, up=up, step=step):
                for n in range(len(chunks)):
                    col_copy(shard, step == 0, up, step, n).wait_send()

    for shard in range(col_devices):
        for present, onward in ((has_next, True), (has_before, False)):

            @pl.when(present)
            def _(shard=shard, onward=onward):
                for n in range(len(chunks)):
                    halo_copy(shard, False, onward, n).wait_send()
                    halo_copy(shard, False, not onward, n).wait_recv()


def product_kernel(
    row_devices, rows, quarter, targets, window, out, blocks, left, filtered, held, bits, sem
):
    span = rows + 2 * RIM
    devices = B // quarter
    r, q = lax.axis_index("row"), lax.axis_index("col")
    base = RIM
    later = [(lo, min(hi, RIM), RIM - lo) for lo, hi in row_chunks(rows) if lo < RIM]

    def fetch(start):
        def go(lo, hi, kinds, part):
            for shard in range(devices):
                copy = pltpu.make_async_copy(
                    window.at[shard, lo:hi, 0:kinds],
                    blocks.at[base + lo : base + hi, 0:kinds, shard * quarter : (shard + 1) * quarter],
                    sem.at[part, shard],
                )
                copy.start() if start else copy.wait()

        go(RIM, RIM + rows, W, 0)

        @pl.when(r > 0)
        def _():
            go(0, RIM, W, 1)

        @pl.when(r < row_devices - 1)
        def _():
            for n, (lo, hi, kinds) in enumerate(later):
                go(RIM + rows + lo, RIM + rows + hi, kinds, 2 + n)

    blocks[0:RIM] = jnp.zeros((RIM,) + blocks.shape[1:], blocks.dtype)
    after = base + RIM + rows
    for lo, hi, kinds in later:
        blocks[after + lo : after + hi, kinds:W] = jnp.zeros((hi - lo, W - kinds, B, B), blocks.dtype)

    @pl.when(r == 0)
    def _():
        blocks[RIM : 2 * RIM] = jnp.zeros((RIM,) + blocks.shape[1:], blocks.dtype)

    @pl.when(r == row_devices - 1)
    def _():
        for lo, hi, kinds in later:
            blocks[after + lo : after + hi, 0:kinds] = jnp.zeros((hi - lo, kinds, B, B), blocks.dtype)

    fetch(True)
    left[...] = jnp.zeros_like(left)
    filtered[...] = jnp.zeros_like(filtered)

    @pl.loop(0, span)
    def _(w):
        row = r * rows - RIM + w
        inside = (row >= 0) & (row < row_devices * rows)
        place = jnp.clip(row, 0, row_devices * rows - 1)
        word = jnp.int32(0)
        for f in range(out.shape[1]):
            target = targets[place, f]
            hit = inside & (target >= 0)
            word = word + jnp.where(hit, lax.shift_left(jnp.int32(1), jnp.where(hit, target - row, 0)), 0)
        bits[w] = word

    fetch(False)

    places = lax.broadcasted_iota(jnp.int32, (quarter, B), 0) + q * quarter
    select = (places == lax.broadcasted_iota(jnp.int32, (quarter, B), 1)).astype(jnp.bfloat16)
    own = pl.ds(pl.multiple_of(q * quarter, quarter), quarter)

    @pl.loop(0, rows)
    def _(i):
        strip = pl.ds(pl.multiple_of(i * quarter, quarter), quarter)
        at = base + RIM + i
        for d in range(W):
            left[at + d, strip, :] = blocks[at, d, own, :]
        for d in range(1, W):
            left[at - d, strip, :] = lax.dot_general(
                select, blocks[at - d, d], NT, preferred_element_type=jnp.float32
            ).astype(jnp.bfloat16)

    half = rows // 2
    full = (0, rows, W, W)
    early, late = (0, half, half, W), (half, rows, W, half)

    def column(lhs, c, shape):
        top, bottom, lows, highs = shape
        strip = slice(top * quarter, bottom * quarter)
        at = base + c
        low_l = jnp.concatenate([lhs[at - d, strip] for d in range(1, lows)], axis=1)
        low_r = jnp.concatenate([blocks[at - d, d] for d in range(1, lows)], axis=0)
        high_l = jnp.concatenate([lhs[at + d, strip] for d in range(highs)], axis=1)
        high_r = jnp.concatenate([blocks[at, d] for d in range(highs)], axis=1)
        total = jnp.dot(low_l, low_r, preferred_element_type=jnp.float32)
        total = total + lax.dot_general(
            high_l, high_r, NT, preferred_element_type=jnp.float32
        )
        return [
            (i, total[(i - top) * quarter : (i - top + 1) * quarter]) for i in range(top, bottom)
        ]

    def square_step(c, shape):
        for i, piece in column(left, c, shape):
            offset = c - RIM - i
            word = bits[jnp.minimum(c, RIM + i)]
            kept = (lax.shift_right_logical(word, jnp.abs(offset)) & 1) != 0
            filtered[base + c, i * quarter : (i + 1) * quarter, :] = jnp.where(
                kept, piece, 0.0
            ).astype(jnp.bfloat16)

            @pl.when((offset >= 0) & (offset < W))
            def _(i=i, piece=piece, offset=offset):
                held[i, offset] = 3.0 * piece

    def cube_step(c, shape):
        for i, piece in column(filtered, c, shape):
            offset = c - RIM - i

            @pl.when((offset >= 0) & (offset < W))
            def _(i=i, piece=piece, offset=offset):
                held[i, offset] = held[i, offset] - 2.0 * piece

    def sweep(lo, hi, body, shape):
        pl.loop(lo, hi)(lambda c: body(c, shape))

    sweep(0, half, square_step, early)
    sweep(half, span - half, square_step, full)
    sweep(span - half, span, square_step, late)
    sweep(RIM, RIM + half, cube_step, (0, half, W, W))
    sweep(RIM + half, span - half, cube_step, full)
    sweep(span - half, span, cube_step, late)

    first = r * rows
    for i in range(rows):
        for f in range(out.shape[1]):
            target = targets[first + i, f]
            there = target >= 0
            offset = jnp.where(there, target - first - i, 0)
            out[i, f] = jnp.where(there, held[i, offset], 0.0)


def per_device(row_devices, col_devices, upper_blocks, block_cols, filter_cols):
    rows, kinds, quarter, _ = upper_blocks.shape
    span = rows + 2 * RIM

    vmem = pl.BlockSpec(memory_space=pltpu.VMEM)
    smem = pl.BlockSpec(memory_space=pltpu.SMEM)
    anywhere = pl.BlockSpec(memory_space=pl.ANY)
    band = pl.pallas_call(
        band_kernel,
        out_shape=jax.ShapeDtypeStruct((rows, W, quarter, B), jnp.bfloat16),
        in_specs=[smem, vmem],
        out_specs=vmem,
        name="band_order",
    )(block_cols, upper_blocks)
    window = pl.pallas_call(
        functools.partial(gather_kernel, row_devices, col_devices),
        out_shape=jax.ShapeDtypeStruct((col_devices, span, W, quarter, B), jnp.bfloat16),
        in_specs=[anywhere],
        out_specs=anywhere,
        scratch_shapes=[
            pltpu.SemaphoreType.DMA,
            pltpu.SemaphoreType.DMA((2, col_devices, rows // 2)),
            pltpu.SemaphoreType.DMA((col_devices, rows // 2)),
            pltpu.SemaphoreType.DMA((2, col_devices, rows // 2)),
            pltpu.SemaphoreType.DMA((2, col_devices, rows // 2)),
        ],
        compiler_params=pltpu.CompilerParams(collective_id=0, has_side_effects=True),
        name="gather_window",
    )(band)
    return pl.pallas_call(
        functools.partial(product_kernel, row_devices, rows, quarter),
        out_shape=jax.ShapeDtypeStruct((rows, filter_cols.shape[1], quarter, B), jnp.float32),
        in_specs=[smem, anywhere],
        out_specs=vmem,
        scratch_shapes=[
            pltpu.VMEM((span + RIM, W, B, B), jnp.bfloat16),
            pltpu.VMEM((span + 2 * RIM, rows * quarter, B), jnp.bfloat16),
            pltpu.VMEM((span + 2 * RIM, rows * quarter, B), jnp.bfloat16),
            pltpu.VMEM((rows, W, quarter, B), jnp.float32),
            pltpu.SMEM((span,), jnp.int32),
            pltpu.SemaphoreType.DMA((2 + rows // 2, col_devices)),
        ],
        compiler_params=pltpu.CompilerParams(vmem_limit_bytes=40 << 20),
        name="products",
    )(filter_cols, window)


def solution(mesh):
    return jax.shard_map(
        functools.partial(per_device, mesh.shape["row"], mesh.shape["col"]),
        mesh=mesh,
        in_specs=(P("row", None, "col", None), P(), P()),
        out_specs=P("row", None, "col", None),
        check_vma=False,
    )
```

time: 86.8 us -> 73.7 us (0.85)
  Pallas kernels: 79.9 us -> 68.6 us
  local copies, waits for them, and re-layouts: 6.37 us -> 4.78 us
    pallas_call x1, Pallas kernels: 53.7 us -> 44.5 us  [per_device(): pl.pallas_call(functools.partial(gather_kernel, row_devices, col_devices)...]
    pallas_call x1, Pallas kernels: 23.7 us -> 21.6 us  [per_device(): pl.pallas_call(functools.partial(product_kernel, row_devices, rows, quart...]
    dynamic_slice x3 -> x0, local copies, waits for them, and re-layouts: 1.6 us -> none  [the longest x2 0.84 us: per_device(): own_filter = lax.dynamic_slice_in_dim(filter_cols, row_first, rows, 0)]
where the time goes in v2:
time: 73.7 us; the launch traced here: 73.4 us
  Pallas kernels  68.6 us (93%)
  local copies, waits for them, and re-layouts  4.78 us (6%)
    pallas_call x1, Pallas kernels, per_device(): pl.pallas_call(functools.partial(gather_kernel, row_devices, col_devices)...  44.5 us
    pallas_call x1, Pallas kernels, per_device(): pl.pallas_call(functools.partial(product_kernel, row_devices, rows, quart...  21.6 us
    unnamed x4, local copies, waits for them, and re-layouts  4.78 us
    pallas_call x1, Pallas kernels, per_device(): pl.pallas_call(band_kernel, out_shape=jax.ShapeDtypeStruct((rows, W, quar...  2.55 us

profile of v2, /device:TPU:1, one launch (start us, length us, event | category | flops | bytes accessed | tf_op | source)
XLA Modules:
  0.0 73.4 jit_solution(4779616351262827544)
XLA Ops:
  0.0 1.4 %copy.4.cols = s32[64,8]{1,0:T(8,128)} copy(s32[64,8]{0,1:T(8,128)} %param.4) | data formatting | bytes 4096 | tf_op args[1]
  1.4 0.8 %copy.5.targets = s32[64,8]{1,0:T(8,128)S(1)} copy(s32[64,8]{0,1:T(8,128)} %param.5) | data formatting | bytes 4096 | tf_op args[2]
  2.2 2.6 %band_order.1.own = bf16[8,8,32,128]{3,2,1,0:T(8,128)(2,1)} custom-call(s32[64,8]{1,0:T(8,128)} %copy.4.cols, bf16[8,8,32,128]{3,2,1,0:T(8,128)(2,1)} %slots.1), custom_call_target="tpu_custom_call" | custom-call | tf_op jit(solution)/shard_map/band_order/pallas_call | solution.py:297
  4.7 44.5 %gather_window.1.window = bf16[4,22,8,32,128]{4,3,2,1,0:T(8,128)(2,1)} custom-call(bf16[8,8,32,128]{3,2,1,0:T(8,128)(2,1)} %band_order.1.own), custom_call_target="tpu_custom_call" | custom-call | tf_op jit(solution)/shard_map/gather_window/pallas_call | solution.py:304
  49.2 0.0 copy-start
  49.2 2.6 %copy-done = bf16[4,22,8,32,128]{4,3,2,1,0:T(8,128)(2,1)S(1)} copy-done((bf16[4,22,8,32,128]{4,3,2,1,0:T(8,128)(2,1)S(1)}, bf16[4,22,8,32,128]{4,3,2,1,0:T(8,128)(2,1)}, u32[]{:S(2)}) %copy-start) | copy-done | bytes 5767192
  51.9 21.6 %products.1 = f32[8,8,32,128]{3,2,1,0:T(8,128)} custom-call(s32[64,8]{1,0:T(8,128)S(1)} %copy.5.targets, bf16[4,22,8,32,128]{4,3,2,1,0:T(8,128)(2,1)S(1)} %copy-done), custom_call_target="tpu_custom_call" | custom-call | tf_op jit(solution)/shard_map/products/pallas_call | solution.py:319
Async XLA Ops:
  49.2 2.6 %copy-start = (bf16[4,22,8,32,128]{4,3,2,1,0:T(8,128)(2,1)S(1)}, bf16[4,22,8,32,128]{4,3,2,1,0:T(8,128)(2,1)}, u32[]{:S(2)}) copy-start(bf16[4,22,8,32,128]{4,3,2,1,0:T(8,128)(2,1)} %gather_window.1.window) | copy-start | bytes 17301508

commit v3 on v2

--- a/solution.py
+++ b/solution.py
@@ -18,24 +18,17 @@
     return [(lo, lo + 2) for lo in reversed(range(0, rows, 2))]
 
 
-def band_kernel(cols, slots, out):
-    rows, kinds = slots.shape[0], slots.shape[1]
-    first = lax.axis_index("row") * rows
-    out[...] = jnp.zeros_like(out)
-    for i in range(rows):
-        for k in range(kinds):
-            column = cols[first + i, k]
-
-            @pl.when(column >= 0)
-            def _(i=i, k=k, column=column):
-                out[i, column - first - i] = slots[i, k]
-
-
 def gather_kernel(
-    row_devices, col_devices, own, window, local_sem, col_send, col_recv, row_send, row_recv
+    row_devices, col_devices, cols, slots, window,
+    table, stored, own, local_sem, col_send, col_recv, row_send, row_recv
 ):
-    rows = own.shape[0]
+    rows, slot_count = slots.shape[0], slots.shape[1]
     r, q = lax.axis_index("row"), lax.axis_index("col")
+    mine = pl.ds(pl.multiple_of(r * rows, rows), rows)
+    table_copy = pltpu.make_async_copy(cols.at[mine], table, local_sem.at[0])
+    slots_copy = pltpu.make_async_copy(slots, stored, local_sem.at[1])
+    table_copy.start()
+    slots_copy.start()
     has_next, has_before = r < row_devices - 1, r > 0
     has_up, has_down = q < col_devices - 1, q > 0
     next_row, before_row = {"row": r + 1}, {"row": r - 1}
@@ -55,9 +48,23 @@
         count = count + present.astype(jnp.int32)
     pl.semaphore_wait(barrier, count)
 
-    local = pltpu.make_async_copy(own, window.at[q, RIM : RIM + rows], local_sem)
-    local.start()
+    local = pltpu.make_async_copy(own, window.at[q, RIM : RIM + rows], local_sem.at[2])
     chunks = row_chunks(rows)
+    table_copy.wait()
+    slots_copy.wait()
+    first = r * rows
+
+    def band_order(lo, hi):
+        for i in range(lo, hi):
+            offsets = [table[i, k] - first - i for k in range(slot_count)]
+            for d in range(W):
+                slot, found = jnp.int32(0), jnp.int32(0)
+                for k in range(slot_count):
+                    hit = offsets[k] == d
+                    slot = jnp.where(hit, k, slot)
+                    found = jnp.where(hit, 1, found)
+                piece = stored[i, slot]
+                own[i, d] = jnp.where(found > 0, piece, jnp.zeros_like(piece))
 
     def source(shard, is_own, lo, hi):
         return own.at[lo:hi] if is_own else window.at[shard, RIM + lo : RIM + hi]
@@ -100,6 +107,7 @@
             halo_copy(shard, is_own, False, n).start()
 
     for n in range(len(chunks)):
+        band_order(*chunks[n])
 
         @pl.when(has_up)
         def _(n=n):
@@ -110,6 +118,8 @@
             col_copy(q, True, False, 0, n).start()
 
         spread(q, True, n)
+
+    local.start()
 
     for step in range(1, col_devices):
         for n in range(len(chunks)):
@@ -151,7 +161,7 @@
 
 
 def product_kernel(
-    row_devices, rows, quarter, targets, window, out, blocks, left, filtered, held, bits, sem
+    row_devices, rows, quarter, filters, window, out, blocks, left, filtered, held, bits, targets, table_sem, sem
 ):
     span = rows + 2 * RIM
     devices = B // quarter
@@ -195,8 +205,11 @@
             blocks[after + lo : after + hi, 0:kinds] = jnp.zeros((hi - lo, kinds, B, B), blocks.dtype)
 
     fetch(True)
+    table_copy = pltpu.make_async_copy(filters, targets, table_sem)
+    table_copy.start()
     left[...] = jnp.zeros_like(left)
     filtered[...] = jnp.zeros_like(filtered)
+    table_copy.wait()
 
     @pl.loop(0, span)
     def _(w):
@@ -292,22 +305,17 @@
     span = rows + 2 * RIM
 
     vmem = pl.BlockSpec(memory_space=pltpu.VMEM)
-    smem = pl.BlockSpec(memory_space=pltpu.SMEM)
     anywhere = pl.BlockSpec(memory_space=pl.ANY)
-    band = pl.pallas_call(
-        band_kernel,
-        out_shape=jax.ShapeDtypeStruct((rows, W, quarter, B), jnp.bfloat16),
-        in_specs=[smem, vmem],
-        out_specs=vmem,
-        name="band_order",
-    )(block_cols, upper_blocks)
     window = pl.pallas_call(
         functools.partial(gather_kernel, row_devices, col_devices),
         out_shape=jax.ShapeDtypeStruct((col_devices, span, W, quarter, B), jnp.bfloat16),
-        in_specs=[anywhere],
+        in_specs=[anywhere, anywhere],
         out_specs=anywhere,
         scratch_shapes=[
-            pltpu.SemaphoreType.DMA,
+            pltpu.SMEM((rows, kinds), jnp.int32),
+            pltpu.VMEM((rows, kinds, quarter, B), jnp.bfloat16),
+            pltpu.VMEM((rows, W, quarter, B), jnp.bfloat16),
+            pltpu.SemaphoreType.DMA((3,)),
             pltpu.SemaphoreType.DMA((2, col_devices, rows // 2)),
             pltpu.SemaphoreType.DMA((col_devices, rows // 2)),
             pltpu.SemaphoreType.DMA((2, col_devices, rows // 2)),
@@ -315,11 +323,11 @@
         ],
         compiler_params=pltpu.CompilerParams(collective_id=0, has_side_effects=True),
         name="gather_window",
-    )(band)
+    )(block_cols, upper_blocks)
     return pl.pallas_call(
         functools.partial(product_kernel, row_devices, rows, quarter),
         out_shape=jax.ShapeDtypeStruct((rows, filter_cols.shape[1], quarter, B), jnp.float32),
-        in_specs=[smem, anywhere],
+        in_specs=[anywhere, anywhere],
         out_specs=vmem,
         scratch_shapes=[
             pltpu.VMEM((span + RIM, W, B, B), jnp.bfloat16),
@@ -327,6 +335,8 @@
             pltpu.VMEM((span + 2 * RIM, rows * quarter, B), jnp.bfloat16),
             pltpu.VMEM((rows, W, quarter, B), jnp.float32),
             pltpu.SMEM((span,), jnp.int32),
+            pltpu.SMEM(filter_cols.shape, jnp.int32),
+            pltpu.SemaphoreType.DMA,
             pltpu.SemaphoreType.DMA((2 + rows // 2, col_devices)),
         ],
         compiler_params=pltpu.CompilerParams(vmem_limit_bytes=40 << 20),

time: 73.7 us -> 70.5 us (0.957)
  Pallas kernels: 68.6 us -> 65.4 us
    pallas_call x1 -> x0, Pallas kernels: 2.55 us -> none  [per_device(): pl.pallas_call(band_kernel, out_shape=jax.ShapeDtypeStruct((rows, W, quar...]
where the time goes in v3:
time: 70.5 us; the launch traced here: 70.2 us
  Pallas kernels  65.4 us (93%)
  local copies, waits for them, and re-layouts  4.78 us (7%)
    pallas_call x1, Pallas kernels, per_device(): pl.pallas_call(functools.partial(gather_kernel, row_devices, col_devices)...  44.5 us
    pallas_call x1, Pallas kernels, per_device(): pl.pallas_call(functools.partial(product_kernel, row_devices, rows, quart...  21 us
    unnamed x4, local copies, waits for them, and re-layouts  4.78 us

profile of v3, /device:TPU:1, one launch (start us, length us, event | category | flops | bytes accessed | tf_op | source)
XLA Modules:
  0.0 70.2 jit_solution(8948246067365556132)
XLA Ops:
  0.0 1.4 %copy.4.cols = s32[64,8]{1,0:T(8,128)} copy(s32[64,8]{0,1:T(8,128)} %param.4) | data formatting | bytes 4096 | tf_op args[1]
  1.4 0.8 %copy.5.filters = s32[64,8]{1,0:T(8,128)S(1)} copy(s32[64,8]{0,1:T(8,128)} %param.5) | data formatting | bytes 4096 | tf_op args[2]
  2.2 44.5 %gather_window.1.window = bf16[4,22,8,32,128]{4,3,2,1,0:T(8,128)(2,1)} custom-call(s32[64,8]{1,0:T(8,128)} %copy.4.cols, bf16[8,8,32,128]{3,2,1,0:T(8,128)(2,1)} %slots.1), custom_call_target="tpu_custom_call" | custom-call | tf_op jit(solution)/shard_map/gather_window/pallas_call | solution.py:309
  46.6 0.0 copy-start
  46.6 2.6 %copy-done = bf16[4,22,8,32,128]{4,3,2,1,0:T(8,128)(2,1)S(1)} copy-done((bf16[4,22,8,32,128]{4,3,2,1,0:T(8,128)(2,1)S(1)}, bf16[4,22,8,32,128]{4,3,2,1,0:T(8,128)(2,1)}, u32[]{:S(2)}) %copy-start) | copy-done | bytes 5767192
  49.3 21.0 %products.1 = f32[8,8,32,128]{3,2,1,0:T(8,128)} custom-call(s32[64,8]{1,0:T(8,128)S(1)} %copy.5.filters, bf16[4,22,8,32,128]{4,3,2,1,0:T(8,128)(2,1)S(1)} %copy-done), custom_call_target="tpu_custom_call" | custom-call | tf_op jit(solution)/shard_map/products/pallas_call | solution.py:327
Async XLA Ops:
  46.6 2.6 %copy-start = (bf16[4,22,8,32,128]{4,3,2,1,0:T(8,128)(2,1)S(1)}, bf16[4,22,8,32,128]{4,3,2,1,0:T(8,128)(2,1)}, u32[]{:S(2)}) copy-start(bf16[4,22,8,32,128]{4,3,2,1,0:T(8,128)(2,1)} %gather_window.1.window) | copy-start | bytes 17301508

commit v4 on v3

--- a/solution.py
+++ b/solution.py
@@ -24,8 +24,7 @@
 ):
     rows, slot_count = slots.shape[0], slots.shape[1]
     r, q = lax.axis_index("row"), lax.axis_index("col")
-    mine = pl.ds(pl.multiple_of(r * rows, rows), rows)
-    table_copy = pltpu.make_async_copy(cols.at[mine], table, local_sem.at[0])
+    table_copy = pltpu.make_async_copy(cols, table, local_sem.at[0])
     slots_copy = pltpu.make_async_copy(slots, stored, local_sem.at[1])
     table_copy.start()
     slots_copy.start()
@@ -56,7 +55,7 @@
 
     def band_order(lo, hi):
         for i in range(lo, hi):
-            offsets = [table[i, k] - first - i for k in range(slot_count)]
+            offsets = [table[k, first + i] - first - i for k in range(slot_count)]
             for d in range(W):
                 slot, found = jnp.int32(0), jnp.int32(0)
                 for k in range(slot_count):
@@ -218,7 +217,7 @@
         place = jnp.clip(row, 0, row_devices * rows - 1)
         word = jnp.int32(0)
         for f in range(out.shape[1]):
-            target = targets[place, f]
+            target = targets[f, place]
             hit = inside & (target >= 0)
             word = word + jnp.where(hit, lax.shift_left(jnp.int32(1), jnp.where(hit, target - row, 0)), 0)
         bits[w] = word
@@ -294,7 +293,7 @@
     first = r * rows
     for i in range(rows):
         for f in range(out.shape[1]):
-            target = targets[first + i, f]
+            target = targets[f, first + i]
             there = target >= 0
             offset = jnp.where(there, target - first - i, 0)
             out[i, f] = jnp.where(there, held[i, offset], 0.0)
@@ -312,7 +311,7 @@
         in_specs=[anywhere, anywhere],
         out_specs=anywhere,
         scratch_shapes=[
-            pltpu.SMEM((rows, kinds), jnp.int32),
+            pltpu.SMEM((kinds, block_cols.shape[0]), jnp.int32),
             pltpu.VMEM((rows, kinds, quarter, B), jnp.bfloat16),
             pltpu.VMEM((rows, W, quarter, B), jnp.bfloat16),
             pltpu.SemaphoreType.DMA((3,)),
@@ -323,7 +322,7 @@
         ],
         compiler_params=pltpu.CompilerParams(collective_id=0, has_side_effects=True),
         name="gather_window",
-    )(block_cols, upper_blocks)
+    )(block_cols.T, upper_blocks)
     return pl.pallas_call(
         functools.partial(product_kernel, row_devices, rows, quarter),
         out_shape=jax.ShapeDtypeStruct((rows, filter_cols.shape[1], quarter, B), jnp.float32),
@@ -335,13 +334,13 @@
             pltpu.VMEM((span + 2 * RIM, rows * quarter, B), jnp.bfloat16),
             pltpu.VMEM((rows, W, quarter, B), jnp.float32),
             pltpu.SMEM((span,), jnp.int32),
-            pltpu.SMEM(filter_cols.shape, jnp.int32),
+            pltpu.SMEM(filter_cols.shape[::-1], jnp.int32),
             pltpu.SemaphoreType.DMA,
             pltpu.SemaphoreType.DMA((2 + rows // 2, col_devices)),
         ],
-        compiler_params=pltpu.CompilerParams(vmem_limit_bytes=40 << 20),
+        compiler_params=pltpu.CompilerParams(vmem_limit_bytes=60 << 20),
         name="products",
-    )(filter_cols, window)
+    )(filter_cols.T, window)
 
 
 def solution(mesh):

time: 70.5 us -> 65.7 us (0.932)
  local copies, waits for them, and re-layouts: 4.78 us -> 0 us
    unnamed x4 -> x0, local copies, waits for them, and re-layouts: 4.78 us -> none
where the time goes in v4:
time: 65.7 us; the launch traced here: 65.5 us
  Pallas kernels  65.5 us (100%)
    pallas_call x1, Pallas kernels, per_device(): pl.pallas_call(functools.partial(gather_kernel, row_devices, col_devices)...  44.5 us
    pallas_call x1, Pallas kernels, per_device(): pl.pallas_call(functools.partial(product_kernel, row_devices, rows, quart...  21.1 us

profile of v4, /device:TPU:1, one launch (start us, length us, event | category | flops | bytes accessed | tf_op | source)
XLA Modules:
  0.0 65.5 jit_solution(12963477488267061185)
XLA Ops:
  0.0 44.5 %gather_window.1.window = bf16[4,22,8,32,128]{4,3,2,1,0:T(8,128)(2,1)} custom-call(s32[8,64]{1,0:T(8,128)} %bitcast.3, bf16[8,8,32,128]{3,2,1,0:T(8,128)(2,1)} %slots.1), custom_call_target="tpu_custom_call" | custom-call | tf_op jit(solution)/shard_map/gather_window/pallas_call | solution.py:308
  44.5 21.1 %products.1 = f32[8,8,32,128]{3,2,1,0:T(8,128)} custom-call(s32[8,64]{1,0:T(8,128)} %bitcast.2, bf16[4,22,8,32,128]{4,3,2,1,0:T(8,128)(2,1)} %gather_window.1.window), custom_call_target="tpu_custom_call" | custom-call | tf_op jit(solution)/shard_map/products/pallas_call | solution.py:326

commit v5 on v4

--- a/solution.py
+++ b/solution.py
@@ -204,6 +204,7 @@
             blocks[after + lo : after + hi, 0:kinds] = jnp.zeros((hi - lo, kinds, B, B), blocks.dtype)
 
     fetch(True)
+    held[:, W] = jnp.zeros((rows, quarter, B), jnp.float32)
     table_copy = pltpu.make_async_copy(filters, targets, table_sem)
     table_copy.start()
     left[...] = jnp.zeros_like(left)
@@ -259,36 +260,43 @@
             (i, total[(i - top) * quarter : (i - top + 1) * quarter]) for i in range(top, bottom)
         ]
 
-    def square_step(c, shape):
-        for i, piece in column(left, c, shape):
+    def slot_of(offset):
+        return jnp.where((offset >= 0) & (offset < W), offset, W)
+
+    def square_step(c, pieces):
+        for i, piece in pieces:
             offset = c - RIM - i
             word = bits[jnp.minimum(c, RIM + i)]
             kept = (lax.shift_right_logical(word, jnp.abs(offset)) & 1) != 0
             filtered[base + c, i * quarter : (i + 1) * quarter, :] = jnp.where(
                 kept, piece, 0.0
             ).astype(jnp.bfloat16)
-
-            @pl.when((offset >= 0) & (offset < W))
-            def _(i=i, piece=piece, offset=offset):
-                held[i, offset] = 3.0 * piece
-
-    def cube_step(c, shape):
-        for i, piece in column(filtered, c, shape):
+            held[i, slot_of(offset)] = 3.0 * piece
+
+    def cube_step(c, pieces):
+        for i, piece in pieces:
             offset = c - RIM - i
-
-            @pl.when((offset >= 0) & (offset < W))
-            def _(i=i, piece=piece, offset=offset):
-                held[i, offset] = held[i, offset] - 2.0 * piece
-
-    def sweep(lo, hi, body, shape):
-        pl.loop(lo, hi)(lambda c: body(c, shape))
-
-    sweep(0, half, square_step, early)
-    sweep(half, span - half, square_step, full)
-    sweep(span - half, span, square_step, late)
-    sweep(RIM, RIM + half, cube_step, (0, half, W, W))
-    sweep(RIM + half, span - half, cube_step, full)
-    sweep(span - half, span, cube_step, late)
+            held[i, slot_of(offset)] = held[i, slot_of(offset)] - 2.0 * piece
+
+    def sweep(lo, hi, lhs, body, shape):
+        pairs = (hi - lo) // 2
+
+        @pl.loop(0, pairs)
+        def _(n):
+            c = lo + 2 * n
+            one, two = column(lhs, c, shape), column(lhs, c + 1, shape)
+            body(c, one)
+            body(c + 1, two)
+
+        if (hi - lo) % 2:
+            body(jnp.int32(hi - 1), column(lhs, hi - 1, shape))
+
+    sweep(0, half, left, square_step, early)
+    sweep(half, span - half, left, square_step, full)
+    sweep(span - half, span, left, square_step, late)
+    sweep(RIM, RIM + half, filtered, cube_step, (0, half, W, W))
+    sweep(RIM + half, span - half, filtered, cube_step, full)
+    sweep(span - half, span, filtered, cube_step, late)
 
     first = r * rows
     for i in range(rows):
@@ -332,7 +340,7 @@
             pltpu.VMEM((span + RIM, W, B, B), jnp.bfloat16),
             pltpu.VMEM((span + 2 * RIM, rows * quarter, B), jnp.bfloat16),
             pltpu.VMEM((span + 2 * RIM, rows * quarter, B), jnp.bfloat16),
-            pltpu.VMEM((rows, W, quarter, B), jnp.float32),
+            pltpu.VMEM((rows, W + 1, quarter, B), jnp.float32),
             pltpu.SMEM((span,), jnp.int32),
             pltpu.SMEM(filter_cols.shape[::-1], jnp.int32),
             pltpu.SemaphoreType.DMA,

time: 65.7 us -> 61.1 us (0.930)
  Pallas kernels: 65.5 us -> 60.9 us
    pallas_call x1, Pallas kernels: 21.1 us -> 16.5 us  [per_device(): pl.pallas_call(functools.partial(product_kernel, row_devices, rows, quart...]
where the time goes in v5:
time: 61.1 us; the launch traced here: 60.9 us
  Pallas kernels  60.9 us (100%)
    pallas_call x1, Pallas kernels, per_device(): pl.pallas_call(functools.partial(gather_kernel, row_devices, col_devices)...  44.5 us
    pallas_call x1, Pallas kernels, per_device(): pl.pallas_call(functools.partial(product_kernel, row_devices, rows, quart...  16.5 us

profile of v5, /device:TPU:1, one launch (start us, length us, event | category | flops | bytes accessed | tf_op | source)
XLA Modules:
  0.0 60.9 jit_solution(18386851036558059969)
XLA Ops:
  0.0 44.5 %gather_window.1.window = bf16[4,22,8,32,128]{4,3,2,1,0:T(8,128)(2,1)} custom-call(s32[8,64]{1,0:T(8,128)} %bitcast.3, bf16[8,8,32,128]{3,2,1,0:T(8,128)(2,1)} %slots.1), custom_call_target="tpu_custom_call" | custom-call | tf_op jit(solution)/shard_map/gather_window/pallas_call | solution.py:316
  44.5 16.5 %products.1 = f32[8,8,32,128]{3,2,1,0:T(8,128)} custom-call(s32[8,64]{1,0:T(8,128)} %bitcast.2, bf16[4,22,8,32,128]{4,3,2,1,0:T(8,128)(2,1)} %gather_window.1.window), custom_call_target="tpu_custom_call" | custom-call | tf_op jit(solution)/shard_map/products/pallas_call | solution.py:334

commit v6 on v5

--- a/solution.py
+++ b/solution.py
@@ -15,7 +15,7 @@
 
 
 def row_chunks(rows):
-    return [(lo, lo + 2) for lo in reversed(range(0, rows, 2))]
+    return [(lo, lo + 1) for lo in reversed(range(rows))]
 
 
 def gather_kernel(
@@ -79,6 +79,9 @@
             device_id_type=MESH,
         )
 
+    def has_halo(onward, n):
+        return chunks[n][1] > rows - RIM if onward else chunks[n][0] < RIM
+
     def halo_copy(shard, is_own, onward, n):
         lo, hi = chunks[n]
         if onward:
@@ -97,13 +100,12 @@
         )
 
     def spread(shard, is_own, n):
-        @pl.when(has_next)
-        def _():
-            halo_copy(shard, is_own, True, n).start()
-
-        @pl.when(has_before)
-        def _():
-            halo_copy(shard, is_own, False, n).start()
+        for present, onward in ((has_next, True), (has_before, False)):
+            if has_halo(onward, n):
+
+                @pl.when(present)
+                def _(onward=onward):
+                    halo_copy(shard, is_own, onward, n).start()
 
     for n in range(len(chunks)):
         band_order(*chunks[n])
@@ -155,8 +157,10 @@
             @pl.when(present)
             def _(shard=shard, onward=onward):
                 for n in range(len(chunks)):
-                    halo_copy(shard, False, onward, n).wait_send()
-                    halo_copy(shard, False, not onward, n).wait_recv()
+                    if has_halo(onward, n):
+                        halo_copy(shard, False, onward, n).wait_send()
+                    if has_halo(not onward, n):
+                        halo_copy(shard, False, not onward, n).wait_recv()
 
 
 def product_kernel(
@@ -229,8 +233,7 @@
     select = (places == lax.broadcasted_iota(jnp.int32, (quarter, B), 1)).astype(jnp.bfloat16)
     own = pl.ds(pl.multiple_of(q * quarter, quarter), quarter)
 
-    @pl.loop(0, rows)
-    def _(i):
+    def left_row(i):
         strip = pl.ds(pl.multiple_of(i * quarter, quarter), quarter)
         at = base + RIM + i
         for d in range(W):
@@ -239,6 +242,11 @@
             left[at - d, strip, :] = lax.dot_general(
                 select, blocks[at - d, d], NT, preferred_element_type=jnp.float32
             ).astype(jnp.bfloat16)
+
+    @pl.loop(0, rows // 2)
+    def _(n):
+        left_row(2 * n)
+        left_row(2 * n + 1)
 
     half = rows // 2
     full = (0, rows, W, W)
@@ -323,10 +331,10 @@
             pltpu.VMEM((rows, kinds, quarter, B), jnp.bfloat16),
             pltpu.VMEM((rows, W, quarter, B), jnp.bfloat16),
             pltpu.SemaphoreType.DMA((3,)),
-            pltpu.SemaphoreType.DMA((2, col_devices, rows // 2)),
-            pltpu.SemaphoreType.DMA((col_devices, rows // 2)),
-            pltpu.SemaphoreType.DMA((2, col_devices, rows // 2)),
-            pltpu.SemaphoreType.DMA((2, col_devices, rows // 2)),
+            pltpu.SemaphoreType.DMA((2, col_devices, rows)),
+            pltpu.SemaphoreType.DMA((col_devices, rows)),
+            pltpu.SemaphoreType.DMA((2, col_devices, rows)),
+            pltpu.SemaphoreType.DMA((2, col_devices, rows)),
         ],
         compiler_params=pltpu.CompilerParams(collective_id=0, has_side_effects=True),
         name="gather_window",
@@ -344,7 +352,7 @@
             pltpu.SMEM((span,), jnp.int32),
             pltpu.SMEM(filter_cols.shape[::-1], jnp.int32),
             pltpu.SemaphoreType.DMA,
-            pltpu.SemaphoreType.DMA((2 + rows // 2, col_devices)),
+            pltpu.SemaphoreType.DMA((2 + rows, col_devices)),
         ],
         compiler_params=pltpu.CompilerParams(vmem_limit_bytes=60 << 20),
         name="products",

time: 61.1 us -> 60.9 us (level)
  no operation moved by 1% of the time
where the time goes in v6:
time: 60.9 us; the launch traced here: 60.7 us
  Pallas kernels  60.7 us (100%)
    pallas_call x1, Pallas kernels, per_device(): pl.pallas_call(functools.partial(gather_kernel, row_devices, col_devices)...  44.8 us
    pallas_call x1, Pallas kernels, per_device(): pl.pallas_call(functools.partial(product_kernel, row_devices, rows, quart...  15.9 us

profile of v6, /device:TPU:1, one launch (start us, length us, event | category | flops | bytes accessed | tf_op | source)
XLA Modules:
  0.0 60.7 jit_solution(12176303278277725419)
XLA Ops:
  0.0 44.8 %gather_window.1.window = bf16[4,22,8,32,128]{4,3,2,1,0:T(8,128)(2,1)} custom-call(s32[8,64]{1,0:T(8,128)} %bitcast.3, bf16[8,8,32,128]{3,2,1,0:T(8,128)(2,1)} %slots.1), custom_call_target="tpu_custom_call" | custom-call | tf_op jit(solution)/shard_map/gather_window/pallas_call | solution.py:324
  44.8 15.9 %products.1 = f32[8,8,32,128]{3,2,1,0:T(8,128)} custom-call(s32[8,64]{1,0:T(8,128)} %bitcast.2, bf16[4,22,8,32,128]{4,3,2,1,0:T(8,128)(2,1)} %gather_window.1.window), custom_call_target="tpu_custom_call" | custom-call | tf_op jit(solution)/shard_map/products/pallas_call | solution.py:342

commit v7 on v6

--- a/solution.py
+++ b/solution.py
@@ -15,7 +15,7 @@
 
 
 def row_chunks(rows):
-    return [(lo, lo + 1) for lo in reversed(range(rows))]
+    return [(lo, lo + 2) for lo in reversed(range(0, rows, 2))]
 
 
 def gather_kernel(
@@ -118,6 +118,7 @@
         def _(n=n):
             col_copy(q, True, False, 0, n).start()
 
+    for n in range(len(chunks)):
         spread(q, True, n)
 
     local.start()

time: 60.9 us -> 61.6 us (1.011)
  Pallas kernels: 60.7 us -> 61.5 us
    pallas_call x1, Pallas kernels: 44.8 us -> 45.5 us  [per_device(): pl.pallas_call(functools.partial(gather_kernel, row_devices, col_devices)...]
where the time goes in v7:
time: 61.6 us; the launch traced here: 61.5 us
  Pallas kernels  61.5 us (100%)
    pallas_call x1, Pallas kernels, per_device(): pl.pallas_call(functools.partial(gather_kernel, row_devices, col_devices)...  45.5 us
    pallas_call x1, Pallas kernels, per_device(): pl.pallas_call(functools.partial(product_kernel, row_devices, rows, quart...  16 us

profile of v7, /device:TPU:1, one launch (start us, length us, event | category | flops | bytes accessed | tf_op | source)
XLA Modules:
  0.0 61.5 jit_solution(4096839486586285530)
XLA Ops:
  0.0 45.5 %gather_window.1.window = bf16[4,22,8,32,128]{4,3,2,1,0:T(8,128)(2,1)} custom-call(s32[8,64]{1,0:T(8,128)} %bitcast.3, bf16[8,8,32,128]{3,2,1,0:T(8,128)(2,1)} %slots.1), custom_call_target="tpu_custom_call" | custom-call | tf_op jit(solution)/shard_map/gather_window/pallas_call | solution.py:325
  45.5 16.0 %products.1 = f32[8,8,32,128]{3,2,1,0:T(8,128)} custom-call(s32[8,64]{1,0:T(8,128)} %bitcast.2, bf16[4,22,8,32,128]{4,3,2,1,0:T(8,128)(2,1)} %gather_window.1.window), custom_call_target="tpu_custom_call" | custom-call | tf_op jit(solution)/shard_map/products/pallas_call | solution.py:343

commit v8 on v7

--- a/solution.py
+++ b/solution.py
@@ -109,6 +109,7 @@
 
     for n in range(len(chunks)):
         band_order(*chunks[n])
+        spread(q, True, n)
 
         @pl.when(has_up)
         def _(n=n):
@@ -117,9 +118,6 @@
         @pl.when(has_down)
         def _(n=n):
             col_copy(q, True, False, 0, n).start()
-
-    for n in range(len(chunks)):
-        spread(q, True, n)
 
     local.start()
 
@@ -133,12 +131,11 @@
                 @pl.when(arrives)
                 def _(shard=shard, up=up, onward=onward, step=step, n=n):
                     col_copy(shard, False, up, step, n).wait_recv()
+                    spread(shard, False, n)
 
                     @pl.when(onward)
                     def _():
                         col_copy(shard, False, up, step, n).start()
-
-                    spread(shard, False, n)
 
     local.wait()
     for step in range(col_devices):

time: 61.6 us -> 61.6 us (level)
  no operation moved by 1% of the time
where the time goes in v8:
time: 61.6 us; the launch traced here: 61.5 us
  Pallas kernels  61.5 us (100%)
    pallas_call x1, Pallas kernels, per_device(): pl.pallas_call(functools.partial(gather_kernel, row_devices, col_devices)...  45.5 us
    pallas_call x1, Pallas kernels, per_device(): pl.pallas_call(functools.partial(product_kernel, row_devices, rows, quart...  16 us

profile of v8, /device:TPU:1, one launch (start us, length us, event | category | flops | bytes accessed | tf_op | source)
XLA Modules:
  0.0 61.5 jit_solution(10856636432784586223)
XLA Ops:
  0.0 45.5 %gather_window.1.window = bf16[4,22,8,32,128]{4,3,2,1,0:T(8,128)(2,1)} custom-call(s32[8,64]{1,0:T(8,128)} %bitcast.3, bf16[8,8,32,128]{3,2,1,0:T(8,128)(2,1)} %slots.1), custom_call_target="tpu_custom_call" | custom-call | tf_op jit(solution)/shard_map/gather_window/pallas_call | solution.py:322
  45.5 16.0 %products.1 = f32[8,8,32,128]{3,2,1,0:T(8,128)} custom-call(s32[8,64]{1,0:T(8,128)} %bitcast.2, bf16[4,22,8,32,128]{4,3,2,1,0:T(8,128)(2,1)} %gather_window.1.window), custom_call_target="tpu_custom_call" | custom-call | tf_op jit(solution)/shard_map/products/pallas_call | solution.py:340
